TPU v7x, 512 devices: a whole 4x8x8 slice. The times are simulated.
512 devices in a mesh: layer: 32 (over y_lo, x, core), plane: 16 (over z, y_hi).
Axes of the slice: x: 4, y: 8 (y_hi: 2, y_lo: 4; y = y_hi * 4 + y_lo), z: 8, core: 2. Of those that a mesh axis runs over, the one named last changes fastest.
Arguments:
- sources: bfloat16 [32, 32, 2, 128, 128], P('layer', 'plane'), may hold values from -6 to 6
- operator_tiles: float32 [32, 384, 2, 128, 128], P('layer', 'plane'), may hold values from -0.109375 to 0.109375
- tile_rows: int32 [32, 384], P('layer', 'plane'), may hold values from 0 to 1, as said below
- tile_cols: int32 [32, 384], P('layer', 'plane'), may hold values from 0 to 5, as said below
- send_blocks: int32 [16, 2, 1], P('plane'), may hold values from 0 to 1
Outputs:
- traces: float32 [32, 32, 2, 128, 128], P('layer', 'plane')
Inputs may be any that keep to these rules, and one draw needn't show every extreme that they name: Entries of tile_rows lie in 0..1; in each layer and plane piece every row block has exactly 12 tiles, and among them at least one reads each of the four parts of the extended trace (arrived blocks, lower neighbour's, upper neighbour's, own trace). Entries of tile_cols index the extended trace of their piece.
All inputs are finite; a program needn't handle non-finite values.
Results may differ from a plain program's by a relative error of at most 0.0003.
Values sent between devices are 32-bit elements; how exact they have to be, the bound alone decides.
A program may use at most 64 MiB of HBM per device.

v0:
```python
import jax
import jax.numpy as jnp
from jax import lax
from jax.sharding import PartitionSpec as P

TICKS = 3


def from_behind(block, axis, distance):
    devices = range(lax.axis_size(axis))
    route = [(i - distance, i) for i in devices if i - distance in devices]
    return lax.ppermute(block, axis, route)


def assemble_operator(mats, rows, cols, blocks_here, extended_count):
    highest = lax.Precision.HIGHEST
    width = mats.shape[-1]
    tile_count = mats.shape[0]
    slots = rows * extended_count + cols
    target = jnp.arange(blocks_here * extended_count, dtype=jnp.int32)
    selector = (slots[None, :] == target[:, None]).astype(jnp.float32)
    flat = mats.reshape(tile_count, 2 * width * width)
    summed = jnp.dot(selector, flat, precision=highest)
    summed = summed.reshape(blocks_here, extended_count, 2, width, width)
    real_part = summed[:, :, 0]
    imag_part = summed[:, :, 1]
    top_row = jnp.stack([real_part, -imag_part], axis=2)
    bottom_row = jnp.stack([imag_part, real_part], axis=2)
    dense = jnp.stack([top_row, bottom_row], axis=1)
    dense = jnp.transpose(dense, (0, 1, 4, 2, 3, 5))
    return dense.reshape(blocks_here * 2 * width, extended_count * 2 * width)


def per_device(sources, operator_tiles, tile_rows, tile_cols, send_blocks):
    highest = lax.Precision.HIGHEST
    source_now = sources[0].astype(jnp.float32)
    mats = operator_tiles[0]
    rows = tile_rows[0]
    cols = tile_cols[0]
    outgoing = send_blocks[0]
    blocks_here = source_now.shape[0]
    width = source_now.shape[2]
    shot_count = source_now.shape[3]
    listed = outgoing.shape[1]
    extended_count = 2 * blocks_here + 2 * listed
    dense = assemble_operator(mats, rows, cols, blocks_here, extended_count)
    traces = jnp.zeros_like(source_now)
    for repeat in range(TICKS):
        arrived = from_behind(traces, "layer", 1)
        to_lower = jnp.take(arrived, outgoing[0], axis=0)
        to_upper = jnp.take(arrived, outgoing[1], axis=0)
        from_lower = from_behind(to_upper, "plane", 1)
        from_upper = from_behind(to_lower, "plane", -1)
        extended = jnp.concatenate([arrived, from_lower, from_upper, traces], axis=0)
        stacked = extended.reshape(extended_count * 2 * width, shot_count)
        fresh = jnp.dot(dense, stacked, precision=highest)
        traces = fresh.reshape(blocks_here, 2, width, shot_count) + source_now
    return traces[None]


def solution(mesh):
    placed = (
        P("layer", "plane", None, None, None),
        P("layer", "plane", None, None, None),
        P("layer", "plane"),
        P("layer", "plane"),
        P("plane", None, None),
    )
    return jax.shard_map(
        per_device,
        mesh=mesh,
        in_specs=placed,
        out_specs=P("layer", "plane", None, None, None),
        check_vma=False,
    )
```

profile of v0, /device:TPU:328, one launch (start us, length us, event | category | flops | bytes accessed | tf_op | source)
XLA Modules:
  0.0 101.3 jit_solution(13641948142534862018)
XLA Ops:
  0.0 1.9 %collective-permute-start = (f32[2,2,128,128]{3,2,1,0:T(8,128)S(1)}, f32[2,2,128,128]{3,2,1,0:T(8,128)}, u32[]{:S(2)}, u32[]{:S(2)}) collective-permute-start(f32[2,2,128,128]{3,2,1,0:T(8,128)S(1)} %broadcast_in_dim.17), channel_id=1, source_target_pairs={{0,16},{16,32},{32,48},{48,64},{64,80},{80,96},{96,112},{112,128},... | collective-permute-start | bytes 786440 | tf_op jit(solution)/shard_map/ppermute | solution.py:12
  2.0 2.9 %reshape_squeeze.3 = f32[24,32768]{1,0:T(8,128)S(1)} reshape(f32[1,24,2,128,128]{4,3,2,1,0:T(8,128)} %param.8) | data formatting | bytes 6291456 | tf_op jit(solution)/shard_map/reshape;squeeze | solution.py:22
  4.9 0.0 copy-start.2
  4.9 0.0 copy-start.3
  4.9 0.5 copy.20
  5.4 0.1 copy-done.2
  5.5 0.0 copy-done.3
  5.5 3.3 %fusion = f32[2,6,2,128,128]{4,1,3,2,0:T(8,128)S(1)} fusion(f32[2,128,128,24]{2,1,0,3:T(8,128)S(1)} %bitcast.81, s32[2,6]{1,0:T(2,128)S(1)} %multiply_add_fusion, s32[24]{0:T(128)S(1)} %add_bitcast_fusion), kind=kOutput, calls=%fused_computation.1 | convolution fusion | flops 113246496 | bytes 4718736 | tf_op jit(solution)/shard_map/dot_general | solution.py:23
  8.8 0.0 copy-start.1
  8.8 0.2 slice_negate_fusion
  9.0 0.4 copy-done.1
  9.5 0.6 fusion.55
  13.7 0.3 maximum_bitcast_fusion.1
  14.0 0.0 collective-permute-done
  14.0 1.0 dynamic-slice_select_fusion.5
  15.0 6.8 %collective-permute-start.2 = (f32[1,2,128,128]{3,2,1,0:T(8,128)S(1)}, f32[1,2,128,128]{3,2,1,0:T(8,128)S(1)}, u32[]{:S(2)}, u32[]{:S(2)}) collective-permute-start(f32[1,2,128,128]{3,2,1,0:T(8,128)S(1)} %get-tuple-element.27), channel_id=1, source_target_pairs={{1,0},{2,1},{3,2},{4,3},{5,4},{6,5},{7,6},{8,7},{9,8},{10,9},{11,1... | collective-permute-start | bytes 393224 | tf_op jit(solution)/shard_map/ppermute | solution.py:12
  21.9 2.9 %collective-permute-start.1 = (f32[1,2,128,128]{3,2,1,0:T(8,128)S(1)}, f32[1,2,128,128]{3,2,1,0:T(8,128)S(1)}, u32[]{:S(2)}, u32[]{:S(2)}) collective-permute-start(f32[1,2,128,128]{3,2,1,0:T(8,128)S(1)} %get-tuple-element.26), channel_id=1, source_target_pairs={{0,1},{1,2},{2,3},{3,4},{4,5},{5,6},{6,7},{7,8},{8,9},{9,10},{10,1... | collective-permute-start | bytes 393224 | tf_op jit(solution)/shard_map/ppermute | solution.py:12
  24.8 0.0 copy-start
  24.8 0.4 maximum_bitcast_fusion
  25.2 3.9 %collective-permute-done.2 = f32[1,2,128,128]{3,2,1,0:T(8,128)S(1)} collective-permute-done((f32[1,2,128,128]{3,2,1,0:T(8,128)S(1)}, f32[1,2,128,128]{3,2,1,0:T(8,128)S(1)}, u32[]{:S(2)}, u32[]{:S(2)}) %collective-permute-start.2) | collective-permute-done | bytes 131104 | tf_op jit(solution)/shard_map/ppermute | solution.py:12
  29.2 8.3 %collective-permute-done.1 = f32[1,2,128,128]{3,2,1,0:T(8,128)S(1)} collective-permute-done((f32[1,2,128,128]{3,2,1,0:T(8,128)S(1)}, f32[1,2,128,128]{3,2,1,0:T(8,128)S(1)}, u32[]{:S(2)}, u32[]{:S(2)}) %collective-permute-start.1) | collective-permute-done | bytes 131104 | tf_op jit(solution)/shard_map/ppermute | solution.py:12
  37.4 0.0 copy-done
  37.4 3.7 %fusion.18 = f32[2,2,128,128]{3,2,1,0:T(8,128)S(1)} fusion(f32[2,2,128,6,2,128]{5,3,2,4,0,1:T(8,128)S(1)} %maximum_bitcast_fusion, f32[2,2,128,128]{3,2,1,0:T(8,128)S(1)} %broadcast_in_dim.17, f32[1,2,128,128]{3,2,1,0:T(8,128)S(1)} %collective-permute-done.2, f32[1,2,128,128]{3,2,1,0:T(8,128)S(1)} %collective-permute-done.1, ...), kind=kOutput, calls=%fused_computation.15 | convolution fusion | flops 1208680448 | bytes 4325376 | tf_op jit(solution)/shard_map/dot_general | solution.py:56
  41.1 2.1 %collective-permute-start.3 = (f32[2,2,128,128]{3,2,1,0:T(8,128)S(1)}, f32[2,2,128,128]{3,2,1,0:T(8,128)S(1)}, u32[]{:S(2)}, u32[]{:S(2)}) collective-permute-start(f32[2,2,128,128]{3,2,1,0:T(8,128)S(1)} %fusion.18), channel_id=1, source_target_pairs={{0,16},{16,32},{32,48},{48,64},{64,80},{80,96},{96,112},{112,128},... | collective-permute-start | bytes 786440 | tf_op jit(solution)/shard_map/ppermute | solution.py:12
  43.2 7.7 %collective-permute-done.3 = f32[2,2,128,128]{3,2,1,0:T(8,128)S(1)} collective-permute-done((f32[2,2,128,128]{3,2,1,0:T(8,128)S(1)}, f32[2,2,128,128]{3,2,1,0:T(8,128)S(1)}, u32[]{:S(2)}, u32[]{:S(2)}) %collective-permute-start.3) | collective-permute-done | bytes 262176 | tf_op jit(solution)/shard_map/ppermute | solution.py:12
  50.9 3.8 %collective-permute-start.5 = (f32[1,2,128,128]{3,2,1,0:T(8,128)S(1)}, f32[1,2,128,128]{3,2,1,0:T(8,128)S(1)}, u32[]{:S(2)}, u32[]{:S(2)}) collective-permute-start(f32[1,2,128,128]{3,2,1,0:T(8,128)S(1)} %get-tuple-element.25), channel_id=1, source_target_pairs={{1,0},{2,1},{3,2},{4,3},{5,4},{6,5},{7,6},{8,7},{9,8},{10,9},{11,1... | collective-permute-start | bytes 393224 | tf_op jit(solution)/shard_map/ppermute | solution.py:12
  54.8 5.9 %collective-permute-start.4 = (f32[1,2,128,128]{3,2,1,0:T(8,128)S(1)}, f32[1,2,128,128]{3,2,1,0:T(8,128)S(1)}, u32[]{:S(2)}, u32[]{:S(2)}) collective-permute-start(f32[1,2,128,128]{3,2,1,0:T(8,128)S(1)} %get-tuple-element.24), channel_id=1, source_target_pairs={{0,1},{1,2},{2,3},{3,4},{4,5},{5,6},{6,7},{7,8},{8,9},{9,10},{10,1... | collective-permute-start | bytes 393224 | tf_op jit(solution)/shard_map/ppermute | solution.py:12
  60.7 4.2 %collective-permute-done.5 = f32[1,2,128,128]{3,2,1,0:T(8,128)S(1)} collective-permute-done((f32[1,2,128,128]{3,2,1,0:T(8,128)S(1)}, f32[1,2,128,128]{3,2,1,0:T(8,128)S(1)}, u32[]{:S(2)}, u32[]{:S(2)}) %collective-permute-start.5) | collective-permute-done | bytes 131104 | tf_op jit(solution)/shard_map/ppermute | solution.py:12
  65.0 2.1 %collective-permute-done.4 = f32[1,2,128,128]{3,2,1,0:T(8,128)S(1)} collective-permute-done((f32[1,2,128,128]{3,2,1,0:T(8,128)S(1)}, f32[1,2,128,128]{3,2,1,0:T(8,128)S(1)}, u32[]{:S(2)}, u32[]{:S(2)}) %collective-permute-start.4) | collective-permute-done | bytes 131104 | tf_op jit(solution)/shard_map/ppermute | solution.py:12
  67.0 2.7 %fusion.21 = f32[2,2,128,128]{3,2,1,0:T(8,128)S(1)} fusion(f32[2,2,128,6,2,128]{5,3,2,4,0,1:T(8,128)S(1)} %maximum_bitcast_fusion, f32[2,2,128,128]{3,2,1,0:T(8,128)S(1)} %fusion.18, f32[1,2,128,128]{3,2,1,0:T(8,128)S(1)} %collective-permute-done.5, f32[1,2,128,128]{3,2,1,0:T(8,128)S(1)} %collective-permute-done.4, ...), kind=kOutput, calls=%fused_computation.16 | convolution fusion | flops 1208680448 | bytes 4325376 | tf_op jit(solution)/shard_map/dot_general | solution.py:56
  69.8 1.9 %collective-permute-start.6 = (f32[2,2,128,128]{3,2,1,0:T(8,128)S(1)}, f32[2,2,128,128]{3,2,1,0:T(8,128)S(1)}, u32[]{:S(2)}, u32[]{:S(2)}) collective-permute-start(f32[2,2,128,128]{3,2,1,0:T(8,128)S(1)} %fusion.21), channel_id=1, source_target_pairs={{0,16},{16,32},{32,48},{48,64},{64,80},{80,96},{96,112},{112,128},... | collective-permute-start | bytes 786440 | tf_op jit(solution)/shard_map/ppermute | solution.py:12
  71.7 7.9 %collective-permute-done.6 = f32[2,2,128,128]{3,2,1,0:T(8,128)S(1)} collective-permute-done((f32[2,2,128,128]{3,2,1,0:T(8,128)S(1)}, f32[2,2,128,128]{3,2,1,0:T(8,128)S(1)}, u32[]{:S(2)}, u32[]{:S(2)}) %collective-permute-start.6) | collective-permute-done | bytes 262176 | tf_op jit(solution)/shard_map/ppermute | solution.py:12
  79.6 5.7 %collective-permute-start.8 = (f32[1,2,128,128]{3,2,1,0:T(8,128)S(1)}, f32[1,2,128,128]{3,2,1,0:T(8,128)S(1)}, u32[]{:S(2)}, u32[]{:S(2)}) collective-permute-start(f32[1,2,128,128]{3,2,1,0:T(8,128)S(1)} %get-tuple-element.23), channel_id=1, source_target_pairs={{1,0},{2,1},{3,2},{4,3},{5,4},{6,5},{7,6},{8,7},{9,8},{10,9},{11,1... | collective-permute-start | bytes 393224 | tf_op jit(solution)/shard_map/ppermute | solution.py:12
  85.3 4.0 %collective-permute-start.7 = (f32[1,2,128,128]{3,2,1,0:T(8,128)S(1)}, f32[1,2,128,128]{3,2,1,0:T(8,128)S(1)}, u32[]{:S(2)}, u32[]{:S(2)}) collective-permute-start(f32[1,2,128,128]{3,2,1,0:T(8,128)S(1)} %get-tuple-element.22), channel_id=1, source_target_pairs={{0,1},{1,2},{2,3},{3,4},{4,5},{5,6},{6,7},{7,8},{8,9},{9,10},{10,1... | collective-permute-start | bytes 393224 | tf_op jit(solution)/shard_map/ppermute | solution.py:12
  89.4 4.7 %collective-permute-done.8 = f32[1,2,128,128]{3,2,1,0:T(8,128)S(1)} collective-permute-done((f32[1,2,128,128]{3,2,1,0:T(8,128)S(1)}, f32[1,2,128,128]{3,2,1,0:T(8,128)S(1)}, u32[]{:S(2)}, u32[]{:S(2)}) %collective-permute-start.8) | collective-permute-done | bytes 131104 | tf_op jit(solution)/shard_map/ppermute | solution.py:12
  94.1 3.8 %collective-permute-done.7 = f32[1,2,128,128]{3,2,1,0:T(8,128)S(1)} collective-permute-done((f32[1,2,128,128]{3,2,1,0:T(8,128)S(1)}, f32[1,2,128,128]{3,2,1,0:T(8,128)S(1)}, u32[]{:S(2)}, u32[]{:S(2)}) %collective-permute-start.7) | collective-permute-done | bytes 131104 | tf_op jit(solution)/shard_map/ppermute | solution.py:12
  97.9 3.5 %fusion.27 = f32[1,2,2,128,128]{4,3,2,1,0:T(8,128)} fusion(f32[2,2,128,6,2,128]{5,3,2,4,0,1:T(8,128)S(1)} %maximum_bitcast_fusion, f32[2,2,128,128]{3,2,1,0:T(8,128)S(1)} %fusion.21, f32[1,2,128,128]{3,2,1,0:T(8,128)S(1)} %collective-permute-done.8, f32[1,2,128,128]{3,2,1,0:T(8,128)S(1)} %collective-permute-done.7, ...), kind=kOutput, calls=%fused_computation.18 | convolution fusion | flops 1208680448 | bytes 4325376 | tf_op jit(solution)/shard_map/dot_general | solution.py:56
  (5 shorter events, 0.1 us)
Async XLA Ops:
  0.0 14.0 %collective-permute-start = (f32[2,2,128,128]{3,2,1,0:T(8,128)S(1)}, f32[2,2,128,128]{3,2,1,0:T(8,128)}, u32[]{:S(2)}, u32[]{:S(2)}) collective-permute-start(f32[2,2,128,128]{3,2,1,0:T(8,128)S(1)} %broadcast_in_dim.17), channel_id=1, source_target_pairs={{0,16},{16,32},{32,48},{48,64},{64,80},{80,96},{96,112},{112,128},... | collective-permute-start | bytes 786440 | tf_op jit(solution)/shard_map/ppermute | solution.py:12
  4.9 0.7 copy-start.2
  4.9 0.7 copy-start.3
  8.8 0.7 copy-start.1
  15.0 14.1 %collective-permute-start.2 = (f32[1,2,128,128]{3,2,1,0:T(8,128)S(1)}, f32[1,2,128,128]{3,2,1,0:T(8,128)S(1)}, u32[]{:S(2)}, u32[]{:S(2)}) collective-permute-start(f32[1,2,128,128]{3,2,1,0:T(8,128)S(1)} %get-tuple-element.27), channel_id=1, source_target_pairs={{1,0},{2,1},{3,2},{4,3},{5,4},{6,5},{7,6},{8,7},{9,8},{10,9},{11,1... | collective-permute-start | bytes 393224 | tf_op jit(solution)/shard_map/ppermute | solution.py:12
  21.9 15.6 %collective-permute-start.1 = (f32[1,2,128,128]{3,2,1,0:T(8,128)S(1)}, f32[1,2,128,128]{3,2,1,0:T(8,128)S(1)}, u32[]{:S(2)}, u32[]{:S(2)}) collective-permute-start(f32[1,2,128,128]{3,2,1,0:T(8,128)S(1)} %get-tuple-element.26), channel_id=1, source_target_pairs={{0,1},{1,2},{2,3},{3,4},{4,5},{5,6},{6,7},{7,8},{8,9},{9,10},{10,1... | collective-permute-start | bytes 393224 | tf_op jit(solution)/shard_map/ppermute | solution.py:12
  24.8 12.6 %copy-start = (bf16[1,2,2,128,128]{4,3,2,1,0:T(8,128)(2,1)S(1)}, bf16[1,2,2,128,128]{4,3,2,1,0:T(8,128)(2,1)}, u32[]{:S(2)}) copy-start(bf16[1,2,2,128,128]{4,3,2,1,0:T(8,128)(2,1)} %param.7) | copy-start | bytes 393220
  41.1 9.8 %collective-permute-start.3 = (f32[2,2,128,128]{3,2,1,0:T(8,128)S(1)}, f32[2,2,128,128]{3,2,1,0:T(8,128)S(1)}, u32[]{:S(2)}, u32[]{:S(2)}) collective-permute-start(f32[2,2,128,128]{3,2,1,0:T(8,128)S(1)} %fusion.18), channel_id=1, source_target_pairs={{0,16},{16,32},{32,48},{48,64},{64,80},{80,96},{96,112},{112,128},... | collective-permute-start | bytes 786440 | tf_op jit(solution)/shard_map/ppermute | solution.py:12
  50.9 14.0 %collective-permute-start.5 = (f32[1,2,128,128]{3,2,1,0:T(8,128)S(1)}, f32[1,2,128,128]{3,2,1,0:T(8,128)S(1)}, u32[]{:S(2)}, u32[]{:S(2)}) collective-permute-start(f32[1,2,128,128]{3,2,1,0:T(8,128)S(1)} %get-tuple-element.25), channel_id=1, source_target_pairs={{1,0},{2,1},{3,2},{4,3},{5,4},{6,5},{7,6},{8,7},{9,8},{10,9},{11,1... | collective-permute-start | bytes 393224 | tf_op jit(solution)/shard_map/ppermute | solution.py:12
  54.8 12.3 %collective-permute-start.4 = (f32[1,2,128,128]{3,2,1,0:T(8,128)S(1)}, f32[1,2,128,128]{3,2,1,0:T(8,128)S(1)}, u32[]{:S(2)}, u32[]{:S(2)}) collective-permute-start(f32[1,2,128,128]{3,2,1,0:T(8,128)S(1)} %get-tuple-element.24), channel_id=1, source_target_pairs={{0,1},{1,2},{2,3},{3,4},{4,5},{5,6},{6,7},{7,8},{8,9},{9,10},{10,1... | collective-permute-start | bytes 393224 | tf_op jit(solution)/shard_map/ppermute | solution.py:12
  69.8 9.8 %collective-permute-start.6 = (f32[2,2,128,128]{3,2,1,0:T(8,128)S(1)}, f32[2,2,128,128]{3,2,1,0:T(8,128)S(1)}, u32[]{:S(2)}, u32[]{:S(2)}) collective-permute-start(f32[2,2,128,128]{3,2,1,0:T(8,128)S(1)} %fusion.21), channel_id=1, source_target_pairs={{0,16},{16,32},{32,48},{48,64},{64,80},{80,96},{96,112},{112,128},... | collective-permute-start | bytes 786440 | tf_op jit(solution)/shard_map/ppermute | solution.py:12
  79.6 14.5 %collective-permute-start.8 = (f32[1,2,128,128]{3,2,1,0:T(8,128)S(1)}, f32[1,2,128,128]{3,2,1,0:T(8,128)S(1)}, u32[]{:S(2)}, u32[]{:S(2)}) collective-permute-start(f32[1,2,128,128]{3,2,1,0:T(8,128)S(1)} %get-tuple-element.23), channel_id=1, source_target_pairs={{1,0},{2,1},{3,2},{4,3},{5,4},{6,5},{7,6},{8,7},{9,8},{10,9},{11,1... | collective-permute-start | bytes 393224 | tf_op jit(solution)/shard_map/ppermute | solution.py:12
  85.3 12.6 %collective-permute-start.7 = (f32[1,2,128,128]{3,2,1,0:T(8,128)S(1)}, f32[1,2,128,128]{3,2,1,0:T(8,128)S(1)}, u32[]{:S(2)}, u32[]{:S(2)}) collective-permute-start(f32[1,2,128,128]{3,2,1,0:T(8,128)S(1)} %get-tuple-element.22), channel_id=1, source_target_pairs={{0,1},{1,2},{2,3},{3,4},{4,5},{5,6},{6,7},{7,8},{8,9},{9,10},{10,1... | collective-permute-start | bytes 393224 | tf_op jit(solution)/shard_map/ppermute | solution.py:12
where the time goes:
time: 102 us; the launch traced here: 101 us
  waiting for transfers between devices  42.7 us (42%)
  starting transfers between devices  35.2 us (35%)
  matrix products  13.1 us (13%)
  local copies, waits for them, and re-layouts  4.58 us (4%)
  between operations  3.82 us (4%)
  other arithmetic  1.98 us (2%)
    ppermute x9, waiting for transfers between devices, from_behind(): return lax.ppermute(block, axis, route)  42.7 us
    ppermute x9, starting transfers between devices, from_behind(): return lax.ppermute(block, axis, route)  35.2 us
    dot_general x3, matrix products, per_device(): fresh = jnp.dot(dense, stacked, precision=highest)  9.87 us
    dot_general x1, matrix products, assemble_operator(): summed = jnp.dot(selector, flat, precision=highest)  3.27 us
    another operation x1, local copies, waits for them, and re-layouts, assemble_operator(): flat = mats.reshape(tile_count, 2 * width * width)  2.88 us
  transfers between devices with their start and end apart: 9, of which 8 were waited for; matrix products, arithmetic and copies ran while one was open for 8% of the time, Pallas kernels for 0%

commit v1 on v0

v1 whole, which is shorter than its diff:
```python
import jax
import jax.numpy as jnp
from jax import lax
from jax.experimental import pallas as pl
from jax.experimental.pallas import tpu as pltpu
from jax.sharding import PartitionSpec as P

MESH = pl.DeviceIdType.MESH
CHUNKS = 2
PAIRS = 3


def lanes_first(shape, half):
    return lax.broadcasted_iota(jnp.int32, shape, len(shape) - 1) < half


def swap_halves(x):
    return pltpu.roll(x, x.shape[-1] // 2, x.ndim - 1)


def kernel(layers, pieces, src_hbm, ops_hbm, rows_hbm, cols_hbm, send_hbm, out_ref,
           src, ops, rows, cols, send, weights, left, first, second, last, picked, arrived, beside, partial,
           in_sem, ops_sem, send_sem, recv_sem):
    layer = lax.axis_index("layer")
    piece = lax.axis_index("plane")
    width = src.shape[-1]
    half = width // 2
    tiles = ops.shape[0]

    has_above = layer > 0
    has_below = layer < layers - 1
    has_lower = piece > 0
    has_upper = piece < pieces - 1
    gives = (jnp.logical_and(has_below, has_lower), jnp.logical_and(has_below, has_upper), has_below)
    takes = (jnp.logical_and(has_above, has_lower), jnp.logical_and(has_above, has_upper), has_above)
    targets = ((layer + 1, piece - 1), (layer + 1, piece + 1), (layer + 1, piece))
    sources = ((layer - 1, piece - 1), (layer - 1, piece + 1), (layer - 1, piece))

    barrier = pltpu.get_barrier_semaphore()
    for take, source in zip(takes, sources):
        @pl.when(take)
        def _():
            pl.semaphore_signal(barrier, inc=1, device_id=source, device_id_type=MESH)

    loads = [
        pltpu.make_async_copy(src_hbm.at[0], src, in_sem.at[0]),
        pltpu.make_async_copy(send_hbm, send, in_sem.at[1]),
        pltpu.make_async_copy(rows_hbm, rows, in_sem.at[2]),
        pltpu.make_async_copy(cols_hbm, cols, in_sem.at[3]),
        pltpu.make_async_copy(ops_hbm.at[0], ops, ops_sem),
    ]
    for load in loads:
        load.start()

    def copies(tick, chunk):
        whole = (first, second)[tick]
        made = []
        for kind in range(3):
            if kind == 2:
                here, there = whole.at[chunk], arrived.at[tick, chunk]
            else:
                here, there = picked.at[tick, chunk, kind], beside.at[tick, chunk, 1 - kind]
            slot = 2 if kind == 2 else 1 - kind
            made.append(pltpu.make_async_remote_copy(
                src_ref=here, dst_ref=there, send_sem=send_sem.at[tick, chunk, kind],
                recv_sem=recv_sem.at[tick, chunk, slot], device_id=targets[kind], device_id_type=MESH))
        return made

    moves = [[copies(tick, chunk) for chunk in range(CHUNKS)] for tick in range(2)]

    def send_out(tick, chunk):
        for kind in range(3):
            @pl.when(gives[kind])
            def _():
                moves[tick][chunk][kind].start()

    def wait_in(tick, chunk, slot):
        kind = 2 if slot == 2 else 1 - slot
        @pl.when(takes[slot])
        def _():
            moves[tick][chunk][kind].wait_recv()

    for slot in range(2):
        @pl.when(jnp.logical_not(takes[slot]))
        def _():
            for tick in range(2):
                for chunk in range(CHUNKS):
                    beside[tick, chunk, slot] = jnp.zeros((width, width), jnp.float32)

    @pl.when(jnp.logical_not(has_above))
    def _():
        arrived[...] = jnp.zeros(arrived.shape, jnp.float32)

    low = lanes_first((width, width), half)
    loads[0].wait()
    for block in range(2):
        real = src[block, 0].astype(jnp.float32)
        imag = src[block, 1].astype(jnp.float32)
        first[0, block] = jnp.where(low, real, swap_halves(imag))
        first[1, block] = jnp.where(low, swap_halves(real), imag)
    loads[1].wait()

    def pick(tick, chunk):
        whole = (first, second)[tick]
        for kind in range(2):
            picked[tick, chunk, kind] = whole[chunk, send[0, kind]]

    for chunk in range(CHUNKS):
        pick(0, chunk)
    @pl.when(has_below)
    def _():
        pl.semaphore_wait(barrier, 1 + has_lower.astype(jnp.int32) + has_upper.astype(jnp.int32))
    for chunk in range(CHUNKS):
        send_out(0, chunk)

    loads[2].wait()
    loads[3].wait()
    for t in range(tiles):
        slot = rows[0, t] * 6 + cols[0, t]
        for s in range(12):
            weights[s, t] = jnp.where(slot == s, 1.0, 0.0).astype(jnp.float32)
    loads[4].wait()

    def assemble(step, carry):
        start = pl.multiple_of(step * 16, 16)
        pieces_of = [ops[t, pl.ds(start, 16)] for t in range(tiles)]
        for s in range(12):
            total = weights[s, 0] * pieces_of[0]
            for t in range(1, tiles):
                total += weights[s, t] * pieces_of[t]
            high = total.astype(jnp.bfloat16)
            rest = (total - high.astype(jnp.float32)).astype(jnp.bfloat16)
            r, c = s // 6, s % 6
            at = pl.multiple_of(r * 2 * width + start, 16)
            left[c // 2, pl.ds(at, 16), pl.ds((c % 2) * width, width)] = high
            left[c // 2, pl.ds(at, 16), pl.ds((2 + c % 2) * width, width)] = rest
        return carry

    lax.fori_loop(0, 2 * width // 16, assemble, 0)

    def product(pair, right, exact):
        right = right.reshape(2 * width, width)
        high = right.astype(jnp.bfloat16)
        out = jnp.dot(left[pair], jnp.concatenate([high, high], axis=0), preferred_element_type=jnp.float32)
        if not exact:
            rest = (right - high.astype(jnp.float32)).astype(jnp.bfloat16)
            out += jnp.dot(left[pair, :, : 2 * width], rest, preferred_element_type=jnp.float32)
        return out

    sign = jnp.where(low, -1.0, 1.0).astype(jnp.float32)

    def finish(total, block, chunk):
        at = block * 2 * width
        return total[at : at + width] + sign * swap_halves(total[at + width : at + 2 * width]) + first[chunk, block]

    for tick in range(2):
        whole = (first, second)[tick]
        exact = tick == 0
        if tick == 0:
            for chunk in range(CHUNKS):
                partial[chunk] = product(2, whole[chunk], exact)
        for chunk in range(CHUNKS):
            wait_in(tick, chunk, 2)
            partial[chunk] += product(0, arrived[tick, chunk], exact)
            wait_in(tick, chunk, 0)
            wait_in(tick, chunk, 1)
            total = partial[chunk] + product(1, beside[tick, chunk], exact)
            for block in range(2):
                (second, last)[tick][chunk, block] = finish(total, block, chunk)
            if tick == 0:
                pick(1, chunk)
                send_out(1, chunk)
                partial[chunk] = product(2, second[chunk], False)

    for block in range(2):
        out_ref[0, block, 0] = jnp.where(low, last[0, block], swap_halves(last[1, block]))
        out_ref[0, block, 1] = jnp.where(low, swap_halves(last[0, block]), last[1, block])

    for tick in range(2):
        for chunk in range(CHUNKS):
            for kind in range(3):
                @pl.when(gives[kind])
                def _():
                    moves[tick][chunk][kind].wait_send()


def solution(mesh):
    layers, pieces = mesh.shape["layer"], mesh.shape["plane"]

    def per_device(sources, operator_tiles, tile_rows, tile_cols, send_blocks):
        tiles, width = operator_tiles.shape[1], operator_tiles.shape[3]
        flat = operator_tiles.reshape(1, tiles, 2 * width, width)
        hbm = pl.BlockSpec(memory_space=pltpu.MemorySpace.HBM)

        def body(*refs):
            kernel(layers, pieces, *refs)

        f32 = jnp.float32
        return pl.pallas_call(
            body,
            out_shape=jax.ShapeDtypeStruct(sources.shape, f32),
            in_specs=[hbm] * 5,
            out_specs=pl.BlockSpec(memory_space=pltpu.VMEM),
            scratch_shapes=[
                pltpu.VMEM(sources.shape[1:], jnp.bfloat16),
                pltpu.VMEM(flat.shape[1:], f32),
                pltpu.SMEM(tile_rows.shape, jnp.int32),
                pltpu.SMEM(tile_cols.shape, jnp.int32),
                pltpu.SMEM((1, 2), jnp.int32),
                pltpu.SMEM((12, tiles), f32),
                pltpu.VMEM((PAIRS, 4 * width, 4 * width), jnp.bfloat16),
                pltpu.VMEM((CHUNKS, 2, width, width), f32),
                pltpu.VMEM((CHUNKS, 2, width, width), f32),
                pltpu.VMEM((CHUNKS, 2, width, width), f32),
                pltpu.VMEM((2, CHUNKS, 2, width, width), f32),
                pltpu.VMEM((2, CHUNKS, 2, width, width), f32),
                pltpu.VMEM((2, CHUNKS, 2, width, width), f32),
                pltpu.VMEM((CHUNKS, 4 * width, width), f32),
                pltpu.SemaphoreType.DMA((4,)),
                pltpu.SemaphoreType.DMA,
                pltpu.SemaphoreType.DMA((2, CHUNKS, 3)),
                pltpu.SemaphoreType.DMA((2, CHUNKS, 3)),
            ],
            compiler_params=pltpu.CompilerParams(collective_id=0, has_side_effects=True),
        )(sources, flat, tile_rows, tile_cols, send_blocks.reshape(1, 2))

    placed = (
        P("layer", "plane", None, None, None),
        P("layer", "plane", None, None, None),
        P("layer", "plane"),
        P("layer", "plane"),
        P("plane", None, None),
    )
    return jax.shard_map(
        per_device, mesh=mesh, in_specs=placed, out_specs=P("layer", "plane", None, None, None), check_vma=False
    )
```

time: 102 us -> 47.8 us (0.47)
  the two profiles are of different devices: /device:TPU:328 before, /device:TPU:201 now
where the time goes in v1:
time: 47.8 us; the launch traced here: 47.6 us
  Pallas kernels  46 us (96%)
  local copies, waits for them, and re-layouts  1.67 us (3%)
    pallas_call x1, Pallas kernels, per_device(): pl.pallas_call(body, out_shape=jax.ShapeDtypeStruct(sources.shape, f32),...  46 us
    unnamed x1, local copies, waits for them, and re-layouts  1.67 us

profile of v1, /device:TPU:201, one launch (start us, length us, event | category | flops | bytes accessed | tf_op | source)
XLA Modules:
  0.0 47.6 jit_solution(3256605693123901107)
XLA Ops:
  0.0 46.0 %shard_map.55 = f32[1,2,2,128,128]{4,3,2,1,0:T(8,128)} custom-call(bf16[1,2,2,128,128]{4,3,2,1,0:T(8,128)(2,1)} %refs_0_.1, f32[1,24,256,128]{3,2,1,0:T(8,128)} %bitcast.2, s32[1,24]{1,0:T(1,128)} %refs_2_.1, s32[1,24]{1,0:T(1,128)} %refs_3_.1, s32[1,2]{1,0:T(1,128)} %bitcast.3), custom_call_target="tpu_custom_call" | custom-call | tf_op jit(solution)/shard_map/pallas_call | solution.py:199
  46.0 1.7 %copy.7 = f32[1,2,2,128,128]{4,3,2,1,0:T(8,128)} copy(f32[1,2,2,128,128]{4,3,2,1,0:T(8,128)} %shard_map.55) | data formatting | bytes 524288

commit v2 on v1

--- a/solution.py
+++ b/solution.py
@@ -8,6 +8,8 @@
 MESH = pl.DeviceIdType.MESH
 CHUNKS = 2
 PAIRS = 3
+RUN = 8
+PASSED = {(0, 0, 1), (0, 1, 1), (1, 0, 1)}
 
 
 def lanes_first(shape, half):
@@ -19,8 +21,8 @@
 
 
 def kernel(layers, pieces, src_hbm, ops_hbm, rows_hbm, cols_hbm, send_hbm, out_ref,
-           src, ops, rows, cols, send, weights, left, first, second, last, picked, arrived, beside, partial,
-           in_sem, ops_sem, send_sem, recv_sem):
+           src, ops, rows, cols, send, weights, left, first, second, last, picked, passed, arrived, beside, partial,
+           in_sem, ops_sem, send_sem, pass_sem, recv_sem):
     layer = lax.axis_index("layer")
     piece = lax.axis_index("plane")
     width = src.shape[-1]
@@ -31,9 +33,24 @@
     has_below = layer < layers - 1
     has_lower = piece > 0
     has_upper = piece < pieces - 1
-    gives = (jnp.logical_and(has_below, has_lower), jnp.logical_and(has_below, has_upper), has_below)
-    takes = (jnp.logical_and(has_above, has_lower), jnp.logical_and(has_above, has_upper), has_above)
+    turns = jnp.logical_and((layer + 1) % RUN == 0, has_below)
+    relays = jnp.logical_and(layer % RUN == 0, has_above)
+    exists = (has_lower, has_upper)
     targets = ((layer + 1, piece - 1), (layer + 1, piece + 1), (layer + 1, piece))
+
+    def both(*conditions):
+        out = conditions[0]
+        for condition in conditions[1:]:
+            out = jnp.logical_and(out, condition)
+        return out
+
+    def gives(tick, chunk, kind):
+        if kind == 2:
+            return has_below
+        out = both(has_below, exists[kind])
+        return both(out, jnp.logical_not(turns)) if (tick, chunk, kind) in PASSED else out
+
+    takes = (both(has_above, has_lower), both(has_above, has_upper), has_above)
     sources = ((layer - 1, piece - 1), (layer - 1, piece + 1), (layer - 1, piece))
 
     barrier = pltpu.get_barrier_semaphore()
@@ -41,6 +58,10 @@
         @pl.when(take)
         def _():
             pl.semaphore_signal(barrier, inc=1, device_id=source, device_id_type=MESH)
+
+    @pl.when(both(relays, has_lower))
+    def _():
+        pl.semaphore_signal(barrier, inc=1, device_id=(layer, piece - 1), device_id_type=MESH)
 
     loads = [
         pltpu.make_async_copy(src_hbm.at[0], src, in_sem.at[0]),
@@ -67,18 +88,38 @@
         return made
 
     moves = [[copies(tick, chunk) for chunk in range(CHUNKS)] for tick in range(2)]
+    relayed = {
+        (tick, chunk, kind): pltpu.make_async_remote_copy(
+            src_ref=passed.at[tick, chunk], dst_ref=beside.at[tick, chunk, 1 - kind], send_sem=pass_sem.at[tick, chunk],
+            recv_sem=recv_sem.at[tick, chunk, 1 - kind], device_id=(layer, piece + 2 * kind - 1), device_id_type=MESH)
+        for tick, chunk, kind in sorted(PASSED)
+    }
 
     def send_out(tick, chunk):
-        for kind in range(3):
-            @pl.when(gives[kind])
+        @pl.when(turns)
+        def _():
+            moves[tick][chunk][2].start()
+        for kind in range(2):
+            @pl.when(gives(tick, chunk, kind))
             def _():
                 moves[tick][chunk][kind].start()
-
-    def wait_in(tick, chunk, slot):
+        @pl.when(both(has_below, jnp.logical_not(turns)))
+        def _():
+            moves[tick][chunk][2].start()
+
+    def wait_in(tick, chunk, slot, only=None):
         kind = 2 if slot == 2 else 1 - slot
-        @pl.when(takes[slot])
+        @pl.when(takes[slot] if only is None else both(takes[slot], only))
         def _():
             moves[tick][chunk][kind].wait_recv()
+
+    def pass_on(tick, chunk):
+        for kind in range(2):
+            if (tick, chunk, kind) in PASSED:
+                @pl.when(both(relays, exists[kind]))
+                def _():
+                    passed[tick, chunk] = jnp.where(send[0, kind] == 0, arrived[tick, chunk, 0], arrived[tick, chunk, 1])
+                    relayed[tick, chunk, kind].start()
 
     for slot in range(2):
         @pl.when(jnp.logical_not(takes[slot]))
@@ -109,9 +150,12 @@
         pick(0, chunk)
     @pl.when(has_below)
     def _():
-        pl.semaphore_wait(barrier, 1 + has_lower.astype(jnp.int32) + has_upper.astype(jnp.int32))
+        pl.semaphore_wait(barrier, 1 + has_lower.astype(jnp.int32) + has_upper.astype(jnp.int32) * (1 + relays.astype(jnp.int32)))
     for chunk in range(CHUNKS):
         send_out(0, chunk)
+
+    wait_in(0, 0, 2, relays)
+    pass_on(0, 0)
 
     loads[2].wait()
     loads[3].wait()
@@ -153,6 +197,9 @@
         at = block * 2 * width
         return total[at : at + width] + sign * swap_halves(total[at + width : at + 2 * width]) + first[chunk, block]
 
+    wait_in(0, 1, 2, relays)
+    pass_on(0, 1)
+
     for tick in range(2):
         whole = (first, second)[tick]
         exact = tick == 0
@@ -160,7 +207,11 @@
             for chunk in range(CHUNKS):
                 partial[chunk] = product(2, whole[chunk], exact)
         for chunk in range(CHUNKS):
-            wait_in(tick, chunk, 2)
+            if tick == 0:
+                wait_in(tick, chunk, 2, jnp.logical_not(relays))
+            else:
+                wait_in(tick, chunk, 2)
+                pass_on(tick, chunk)
             partial[chunk] += product(0, arrived[tick, chunk], exact)
             wait_in(tick, chunk, 0)
             wait_in(tick, chunk, 1)
@@ -179,9 +230,13 @@
     for tick in range(2):
         for chunk in range(CHUNKS):
             for kind in range(3):
-                @pl.when(gives[kind])
+                @pl.when(gives(tick, chunk, kind))
                 def _():
                     moves[tick][chunk][kind].wait_send()
+    for tick, chunk, kind in sorted(PASSED):
+        @pl.when(both(relays, exists[kind]))
+        def _():
+            relayed[tick, chunk, kind].wait_send()
 
 
 def solution(mesh):
@@ -198,7 +253,7 @@
         f32 = jnp.float32
         return pl.pallas_call(
             body,
-            out_shape=jax.ShapeDtypeStruct(sources.shape, f32),
+            out_shape=pltpu.VMEM(sources.shape, f32),
             in_specs=[hbm] * 5,
             out_specs=pl.BlockSpec(memory_space=pltpu.VMEM),
             scratch_shapes=[
@@ -213,12 +268,14 @@
                 pltpu.VMEM((CHUNKS, 2, width, width), f32),
                 pltpu.VMEM((CHUNKS, 2, width, width), f32),
                 pltpu.VMEM((2, CHUNKS, 2, width, width), f32),
+                pltpu.VMEM((2, CHUNKS, width, width), f32),
                 pltpu.VMEM((2, CHUNKS, 2, width, width), f32),
                 pltpu.VMEM((2, CHUNKS, 2, width, width), f32),
                 pltpu.VMEM((CHUNKS, 4 * width, width), f32),
                 pltpu.SemaphoreType.DMA((4,)),
                 pltpu.SemaphoreType.DMA,
                 pltpu.SemaphoreType.DMA((2, CHUNKS, 3)),
+                pltpu.SemaphoreType.DMA((2, CHUNKS)),
                 pltpu.SemaphoreType.DMA((2, CHUNKS, 3)),
             ],
             compiler_params=pltpu.CompilerParams(collective_id=0, has_side_effects=True),

time: 47.8 us -> 40.2 us (0.84)
  the two profiles are of different devices: /device:TPU:201 before, /device:TPU:264 now
where the time goes in v2:
time: 40.2 us; the launch traced here: 40.1 us
  Pallas kernels  39.4 us (98%)
  local copies, waits for them, and re-layouts  0.71 us (2%)
    pallas_call x1, Pallas kernels, per_device(): pl.pallas_call(body, out_shape=pltpu.VMEM(sources.shape, f32), in_specs=[...  39.4 us

profile of v2, /device:TPU:264, one launch (start us, length us, event | category | flops | bytes accessed | tf_op | source)
XLA Modules:
  0.0 40.1 jit_solution(3124592077662477309)
XLA Ops:
  0.0 39.4 %shard_map.55 = f32[1,2,2,128,128]{4,3,2,1,0:T(8,128)S(1)} custom-call(bf16[1,2,2,128,128]{4,3,2,1,0:T(8,128)(2,1)} %refs_0_.1, f32[1,24,256,128]{3,2,1,0:T(8,128)} %bitcast.2, s32[1,24]{1,0:T(1,128)} %refs_2_.1, s32[1,24]{1,0:T(1,128)} %refs_3_.1, s32[1,2]{1,0:T(1,128)} %bitcast.3), custom_call_target="tpu_custom_call" | custom-call | tf_op jit(solution)/shard_map/pallas_call | solution.py:254
  39.4 0.7 %copy.7 = f32[1,2,2,128,128]{4,3,2,1,0:T(8,128)} copy(f32[1,2,2,128,128]{4,3,2,1,0:T(8,128)S(1)} %shard_map.55) | data formatting | bytes 524288

commit v3 on v1

--- a/solution.py
+++ b/solution.py
@@ -8,6 +8,8 @@
 MESH = pl.DeviceIdType.MESH
 CHUNKS = 2
 PAIRS = 3
+RUN = 8
+LONG = {(0, 0): (7, 15, 23), (0, 1): (7, 15, 23), (1, 0): (23,)}
 
 
 def lanes_first(shape, half):
@@ -19,8 +21,8 @@
 
 
 def kernel(layers, pieces, src_hbm, ops_hbm, rows_hbm, cols_hbm, send_hbm, out_ref,
-           src, ops, rows, cols, send, weights, left, first, second, last, picked, arrived, beside, partial,
-           in_sem, ops_sem, send_sem, recv_sem):
+           src, ops, rows, cols, send, weights, left, first, second, last, picked, passed, arrived, beside, partial,
+           in_sem, ops_sem, send_sem, pass_sem, long_sem, recv_sem):
     layer = lax.axis_index("layer")
     piece = lax.axis_index("plane")
     width = src.shape[-1]
@@ -31,9 +33,48 @@
     has_below = layer < layers - 1
     has_lower = piece > 0
     has_upper = piece < pieces - 1
-    gives = (jnp.logical_and(has_below, has_lower), jnp.logical_and(has_below, has_upper), has_below)
-    takes = (jnp.logical_and(has_above, has_lower), jnp.logical_and(has_above, has_upper), has_above)
+    turns = jnp.logical_and((layer + 1) % RUN == 0, has_below)
+    lands = jnp.logical_and(layer % RUN == 0, has_above)
+    stands = jnp.logical_and((layer + 1) % RUN == 0, layer != 2 * RUN - 1)
+
+    def long_way(of_layer, of_piece, back):
+        crossing = of_layer == (RUN - 1 if back else 3 * RUN - 1)
+        other = of_piece + 1 - 2 * (of_piece % 2)
+        there = jnp.where(crossing, (3 * RUN if back else RUN) - 1, of_layer + (-2 if back else 2) * RUN)
+        return there, jnp.where(crossing, other, of_piece)
+
+    helper = long_way(layer, piece, False)
+    helped = long_way(layer, piece, True)
+    helps = jnp.logical_and(stands, helped[1] < pieces - 1)
+    landing = long_way(layer - 1, piece - 1, False)
+    exists = (has_lower, has_upper)
     targets = ((layer + 1, piece - 1), (layer + 1, piece + 1), (layer + 1, piece))
+
+    def both(*conditions):
+        out = conditions[0]
+        for condition in conditions[1:]:
+            out = jnp.logical_and(out, condition)
+        return out
+
+    def among(which, layers_named):
+        out = which == layers_named[0]
+        for named in layers_named[1:]:
+            out = jnp.logical_or(out, which == named)
+        return out
+
+    def goes_long(tick, chunk):
+        return among(layer, LONG[tick, chunk])
+
+    def helps_long(tick, chunk):
+        return both(helps, among(helped[0], LONG[tick, chunk]))
+
+    def gives(tick, chunk, kind):
+        if kind == 2:
+            return has_below
+        out = both(has_below, exists[kind])
+        return both(out, jnp.logical_not(goes_long(tick, chunk))) if kind == 1 and (tick, chunk) in LONG else out
+
+    takes = (both(has_above, has_lower), both(has_above, has_upper), has_above)
     sources = ((layer - 1, piece - 1), (layer - 1, piece + 1), (layer - 1, piece))
 
     barrier = pltpu.get_barrier_semaphore()
@@ -41,6 +82,14 @@
         @pl.when(take)
         def _():
             pl.semaphore_signal(barrier, inc=1, device_id=source, device_id_type=MESH)
+
+    @pl.when(both(lands, has_lower))
+    def _():
+        pl.semaphore_signal(barrier, inc=1, device_id=landing, device_id_type=MESH)
+
+    @pl.when(helps)
+    def _():
+        pl.semaphore_signal(barrier, inc=1, device_id=helped, device_id_type=MESH)
 
     loads = [
         pltpu.make_async_copy(src_hbm.at[0], src, in_sem.at[0]),
@@ -67,10 +116,22 @@
         return made
 
     moves = [[copies(tick, chunk) for chunk in range(CHUNKS)] for tick in range(2)]
+    sent_long, passed_on = {}, {}
+    for at, (tick, chunk) in enumerate(LONG):
+        sent_long[tick, chunk] = pltpu.make_async_remote_copy(
+            src_ref=picked.at[tick, chunk, 1], dst_ref=passed.at[at], send_sem=send_sem.at[tick, chunk, 1],
+            recv_sem=long_sem.at[at], device_id=helper, device_id_type=MESH)
+        passed_on[tick, chunk] = pltpu.make_async_remote_copy(
+            src_ref=passed.at[at], dst_ref=beside.at[tick, chunk, 0], send_sem=pass_sem.at[at],
+            recv_sem=recv_sem.at[tick, chunk, 0], device_id=(helped[0] + 1, helped[1] + 1), device_id_type=MESH)
 
     def send_out(tick, chunk):
+        if (tick, chunk) in LONG:
+            @pl.when(both(goes_long(tick, chunk), has_upper))
+            def _():
+                sent_long[tick, chunk].start()
         for kind in range(3):
-            @pl.when(gives[kind])
+            @pl.when(gives(tick, chunk, kind))
             def _():
                 moves[tick][chunk][kind].start()
 
@@ -79,6 +140,13 @@
         @pl.when(takes[slot])
         def _():
             moves[tick][chunk][kind].wait_recv()
+
+    def pass_on(tick, chunk):
+        if (tick, chunk) in LONG:
+            @pl.when(helps_long(tick, chunk))
+            def _():
+                sent_long[tick, chunk].wait_recv()
+                passed_on[tick, chunk].start()
 
     for slot in range(2):
         @pl.when(jnp.logical_not(takes[slot]))
@@ -107,11 +175,18 @@
 
     for chunk in range(CHUNKS):
         pick(0, chunk)
-    @pl.when(has_below)
+    def count(condition):
+        return condition.astype(jnp.int32)
+
+    below = count(has_below) * (1 + count(has_lower) + count(has_upper)) + count(both(turns, has_upper)) + count(helps)
+
+    @pl.when(below > 0)
     def _():
-        pl.semaphore_wait(barrier, 1 + has_lower.astype(jnp.int32) + has_upper.astype(jnp.int32))
+        pl.semaphore_wait(barrier, below)
     for chunk in range(CHUNKS):
         send_out(0, chunk)
+
+    pass_on(0, 0)
 
     loads[2].wait()
     loads[3].wait()
@@ -153,7 +228,12 @@
         at = block * 2 * width
         return total[at : at + width] + sign * swap_halves(total[at + width : at + 2 * width]) + first[chunk, block]
 
+    pass_on(0, 1)
+
     for tick in range(2):
+        if tick == 1:
+            pass_on(1, 0)
+            pass_on(1, 1)
         whole = (first, second)[tick]
         exact = tick == 0
         if tick == 0:
@@ -179,9 +259,16 @@
     for tick in range(2):
         for chunk in range(CHUNKS):
             for kind in range(3):
-                @pl.when(gives[kind])
+                @pl.when(gives(tick, chunk, kind))
                 def _():
                     moves[tick][chunk][kind].wait_send()
+    for tick, chunk in LONG:
+        @pl.when(both(goes_long(tick, chunk), has_upper))
+        def _():
+            sent_long[tick, chunk].wait_send()
+        @pl.when(helps_long(tick, chunk))
+        def _():
+            passed_on[tick, chunk].wait_send()
 
 
 def solution(mesh):
@@ -198,7 +285,7 @@
         f32 = jnp.float32
         return pl.pallas_call(
             body,
-            out_shape=jax.ShapeDtypeStruct(sources.shape, f32),
+            out_shape=pltpu.VMEM(sources.shape, f32),
             in_specs=[hbm] * 5,
             out_specs=pl.BlockSpec(memory_space=pltpu.VMEM),
             scratch_shapes=[
@@ -213,12 +300,15 @@
                 pltpu.VMEM((CHUNKS, 2, width, width), f32),
                 pltpu.VMEM((CHUNKS, 2, width, width), f32),
                 pltpu.VMEM((2, CHUNKS, 2, width, width), f32),
+                pltpu.VMEM((len(LONG), width, width), f32),
                 pltpu.VMEM((2, CHUNKS, 2, width, width), f32),
                 pltpu.VMEM((2, CHUNKS, 2, width, width), f32),
                 pltpu.VMEM((CHUNKS, 4 * width, width), f32),
                 pltpu.SemaphoreType.DMA((4,)),
                 pltpu.SemaphoreType.DMA,
                 pltpu.SemaphoreType.DMA((2, CHUNKS, 3)),
+                pltpu.SemaphoreType.DMA((len(LONG),)),
+                pltpu.SemaphoreType.DMA((len(LONG),)),
                 pltpu.SemaphoreType.DMA((2, CHUNKS, 3)),
             ],
             compiler_params=pltpu.CompilerParams(collective_id=0, has_side_effects=True),

time: 47.8 us -> 38.5 us (0.81)
  the two profiles are of different devices: /device:TPU:201 before, /device:TPU:233 now
where the time goes in v3:
time: 38.5 us; the launch traced here: 38.4 us
  Pallas kernels  37.7 us (98%)
  local copies, waits for them, and re-layouts  0.71 us (2%)
    pallas_call x1, Pallas kernels, per_device(): pl.pallas_call(body, out_shape=pltpu.VMEM(sources.shape, f32), in_specs=[...  37.7 us

profile of v3, /device:TPU:233, one launch (start us, length us, event | category | flops | bytes accessed | tf_op | source)
XLA Modules:
  0.0 38.4 jit_solution(126454012021942638)
XLA Ops:
  0.0 37.7 %shard_map.55 = f32[1,2,2,128,128]{4,3,2,1,0:T(8,128)S(1)} custom-call(bf16[1,2,2,128,128]{4,3,2,1,0:T(8,128)(2,1)} %refs_0_.1, f32[1,24,256,128]{3,2,1,0:T(8,128)} %bitcast.2, s32[1,24]{1,0:T(1,128)} %refs_2_.1, s32[1,24]{1,0:T(1,128)} %refs_3_.1, s32[1,2]{1,0:T(1,128)} %bitcast.3), custom_call_target="tpu_custom_call" | custom-call | tf_op jit(solution)/shard_map/pallas_call | solution.py:286
  37.7 0.7 %copy.7 = f32[1,2,2,128,128]{4,3,2,1,0:T(8,128)} copy(f32[1,2,2,128,128]{4,3,2,1,0:T(8,128)S(1)} %shard_map.55) | data formatting | bytes 524288

commit v4 on v3

--- a/solution.py
+++ b/solution.py
@@ -130,7 +130,7 @@
             @pl.when(both(goes_long(tick, chunk), has_upper))
             def _():
                 sent_long[tick, chunk].start()
-        for kind in range(3):
+        for kind in (2, 0, 1):
             @pl.when(gives(tick, chunk, kind))
             def _():
                 moves[tick][chunk][kind].start()

time: 38.5 us -> 38.5 us (level)
  no operation moved by 1% of the time
where the time goes in v4:
time: 38.5 us; the launch traced here: 38.4 us
  Pallas kernels  37.7 us (98%)
  local copies, waits for them, and re-layouts  0.71 us (2%)
    pallas_call x1, Pallas kernels, per_device(): pl.pallas_call(body, out_shape=pltpu.VMEM(sources.shape, f32), in_specs=[...  37.7 us

profile of v4, /device:TPU:233, one launch (start us, length us, event | category | flops | bytes accessed | tf_op | source)
XLA Modules:
  0.0 38.4 jit_solution(4697022486660492260)
XLA Ops:
  0.0 37.7 %shard_map.55 = f32[1,2,2,128,128]{4,3,2,1,0:T(8,128)S(1)} custom-call(bf16[1,2,2,128,128]{4,3,2,1,0:T(8,128)(2,1)} %refs_0_.1, f32[1,24,256,128]{3,2,1,0:T(8,128)} %bitcast.2, s32[1,24]{1,0:T(1,128)} %refs_2_.1, s32[1,24]{1,0:T(1,128)} %refs_3_.1, s32[1,2]{1,0:T(1,128)} %bitcast.3), custom_call_target="tpu_custom_call" | custom-call | tf_op jit(solution)/shard_map/pallas_call | solution.py:286
  37.7 0.7 %copy.7 = f32[1,2,2,128,128]{4,3,2,1,0:T(8,128)} copy(f32[1,2,2,128,128]{4,3,2,1,0:T(8,128)S(1)} %shard_map.55) | data formatting | bytes 524288
